TPU v7x, 32 devices: a whole 2x2x4 slice. The times are simulated.
32 devices in a mesh: scan: 4 (over y, x), slab: 8 (over z, core).
Axes of the slice: x: 2, y: 2, z: 4, core: 2. Of those that a mesh axis runs over, the one named last changes fastest.
Arguments:
- solution: float32 [1536, 2048], P(('scan', 'slab')), parts along dimension 0, may hold values from -6 to 6
- direction: float32 [1536, 2048], P(('scan', 'slab')), parts along dimension 0, may hold values from -20 to 20
- gradient: float32 [1536, 2048], P(('scan', 'slab')), parts along dimension 0, may hold values from -40 to 40
- residual: float32 [512, 64, 896], P(('scan', 'slab')), parts along dimension 0, may hold values from -20 to 20
- tiles: bfloat16 [4, 2048, 896], replicated, may hold values from -0.125 to 0.125
- offsets: int32 [512], P(('scan', 'slab')), parts along dimension 0, may hold values from 1 to 320, as said below
Outputs:
- solution_next: float32 [1536, 2048], P(('scan', 'slab')), parts along dimension 0
- residual_next: float32 [512, 64, 896], P(('scan', 'slab')), parts along dimension 0
- gradient_next: float32 [1536, 2048], P(('scan', 'slab')), parts along dimension 0
- direction_next: float32 [1536, 2048], P(('scan', 'slab')), parts along dimension 0
There are 4 independent parts, one for each index of `scan`. A program takes and returns all parts, laid end to end along the dimension named above; an argument that names none is the same for every part. Nothing has to cross between parts.
Inputs may be any that keep to these rules, and one draw needn't show every extreme that they name: View v belongs to slab v // 16, whose planes are s * 48 to s * 48 + 47 for slab s; its window offsets[v] to offsets[v] + 63 meets that slab and lies within the slab before it, the slab itself and the slab after it; offsets are 1 or more.
All inputs are finite; a program needn't handle non-finite values.
Results may differ from a plain program's by a relative error of at most 0.0029.
Values may be sent and summed in bfloat16 or wider, within the bound.
A program may use at most 192 MiB of HBM per device.

v0:
```python
import jax
import jax.numpy as jnp
from jax import lax
from jax.sharding import PartitionSpec as P

ANGLES = 4


def with_halo(block, sides, width):
    for axis, dim in sides:
        count = lax.axis_size(axis)
        forward = [(i, i + 1) for i in range(count - 1)]
        backward = [(target, source) for source, target in forward]
        low = lax.ppermute(
            lax.slice_in_dim(block, block.shape[dim] - width, None, axis=dim), axis, forward
        )
        high = lax.ppermute(lax.slice_in_dim(block, 0, width, axis=dim), axis, backward)
        block = jnp.concatenate([low, block, high], axis=dim)
    return block


def from_behind(block, axis, distance):
    devices = range(lax.axis_size(axis))
    route = [(i - distance, i) for i in devices if i - distance in devices]
    return lax.ppermute(block, axis, route)


def project(volume_rows, firsts, tiles, detector_rows):

    def take_window(first_row):
        return lax.dynamic_slice_in_dim(volume_rows, first_row, detector_rows, 0)

    windows = jax.vmap(take_window)(firsts)
    grouped = windows.reshape(-1, ANGLES, detector_rows, windows.shape[-1])
    images = jnp.einsum("gkir,krc->gkic", grouped, tiles, preferred_element_type=jnp.float32)
    return images.reshape(windows.shape[0], detector_rows, tiles.shape[2])


def backproject(accumulated, firsts, sinogram, tiles):
    detector_rows = sinogram.shape[1]
    grouped = sinogram.reshape(-1, ANGLES, detector_rows, sinogram.shape[2])
    contribution = jnp.einsum("gkic,krc->gkir", grouped, tiles, preferred_element_type=jnp.float32)
    contribution = contribution.reshape(sinogram.shape[0] * detector_rows, tiles.shape[1])
    target_rows = (firsts[:, None] + jnp.arange(detector_rows, dtype=jnp.int32)[None, :]).reshape(
        -1
    )
    return accumulated.at[target_rows].add(contribution)


def local(solution, direction, gradient, residual, tiles, offsets):
    slab_rows = solution.shape[0]
    plane_cells = solution.shape[1]
    detector_rows = residual.shape[1]
    slab_index = lax.axis_index("slab")
    slab_start = slab_index * slab_rows
    direction_half = direction.astype(jnp.bfloat16)
    grad_part = jnp.sum(gradient * gradient)
    grad_norm = lax.psum(grad_part, "slab")
    nearby = with_halo(direction_half, (("slab", 0),), slab_rows)
    own_firsts = offsets - slab_start + slab_rows
    projected = project(nearby, own_firsts, tiles, detector_rows)
    image_part = jnp.sum(projected * projected)
    image_norm = lax.psum(image_part, "slab")
    step_size = grad_norm / image_norm
    solution_next = solution + step_size * direction
    residual_next = residual - step_size * projected
    residual_half = residual_next.astype(jnp.bfloat16)
    accumulated = backproject(
        jnp.zeros((3 * slab_rows, plane_cells), jnp.float32), own_firsts, residual_half, tiles
    )
    from_above = from_behind(accumulated[:slab_rows], "slab", -1)
    from_below = from_behind(accumulated[2 * slab_rows :], "slab", 1)
    gradient_next = accumulated[slab_rows : 2 * slab_rows] + from_above + from_below
    new_norm = lax.psum(jnp.sum(gradient_next * gradient_next), "slab")
    direction_next = gradient_next + new_norm / grad_norm * direction
    return (solution_next, residual_next, gradient_next, direction_next)


def solution(mesh):
    placed = (
        P(("scan", "slab"), None),
        P(("scan", "slab"), None),
        P(("scan", "slab"), None),
        P(("scan", "slab"), None, None),
        P(),
        P(("scan", "slab")),
    )
    return jax.shard_map(
        local,
        mesh=mesh,
        in_specs=placed,
        out_specs=(
            P(("scan", "slab"), None),
            P(("scan", "slab"), None, None),
            P(("scan", "slab"), None),
            P(("scan", "slab"), None),
        ),
        check_vma=False,
    )
```

profile of v0, /device:TPU:0, one launch (start us, length us, event | category | flops | bytes accessed | tf_op | source)
XLA Modules:
  0.0 147.9 jit_solution(391435288854549811)
XLA Ops:
  1.7 2.4 %collective-permute-start = (bf16[48,2048]{1,0:T(8,128)(2,1)S(1)}, bf16[48,2048]{1,0:T(8,128)(2,1)S(1)}, u32[]{:S(2)}, u32[]{:S(2)}) collective-permute-start(bf16[48,2048]{1,0:T(8,128)(2,1)S(1)} %convert_element_type.6), channel_id=1, source_target_pairs={{0,1},{1,2},{2,3},{3,4},{4,5},{5,6},{6,7},{8,9},{9,10},{10,11},{11... | collective-permute-start | bytes 589832 | tf_op jit(solution)/shard_map/ppermute | solution.py:14
  5.4 1.7 %multiply_reduce_fusion.2 = f32[]{:T(128)} fusion(f32[48,2048]{1,0:T(8,128)} %param.8), kind=kLoop, calls=%fused_computation.21 | loop fusion | flops 196607 | bytes 393220 | tf_op jit(solution)/shard_map/reduce_sum | solution.py:57
  7.9 1.6 %collective-permute-done.1 = bf16[48,2048]{1,0:T(8,128)(2,1)S(1)} collective-permute-done((bf16[48,2048]{1,0:T(8,128)(2,1)S(1)}, bf16[48,2048]{1,0:T(8,128)(2,1)S(1)}, u32[]{:S(2)}, u32[]{:S(2)}) %collective-permute-start.1) | collective-permute-done | bytes 196640 | tf_op jit(solution)/shard_map/ppermute | solution.py:17
  9.6 32.2 %while.1 = (s32[]{:T(128)}, bf16[144,2048]{1,0:T(8,128)(2,1)S(1)}, s32[16,2]{0,1:T(2,128)S(1)}, bf16[16,64,2048]{2,1,0:T(8,128)(2,1)}, s32[]{:T(128)}) while((s32[]{:T(128)}, bf16[144,2048]{1,0:T(8,128)(2,1)S(1)}, s32[16,2]{0,1:T(2,128)S(1)}, bf16[16,64,2048]{2,1,0:T(8,128)(2,1)}, s32[]{:T(128)}) %tuple.26), condition=%wide.while_cond, body=%wide.while_body.sunk | while | flops 2 | bytes 525401 | solution.py:31
  16.2 1.4 bitcast_dynamic-update-slice_fusion.2
  18.2 1.4 bitcast_dynamic-update-slice_fusion.2
  20.3 1.4 bitcast_dynamic-update-slice_fusion.2
  24.3 1.4 bitcast_dynamic-update-slice_fusion.2
  26.3 1.4 bitcast_dynamic-update-slice_fusion.2
  30.3 1.4 bitcast_dynamic-update-slice_fusion.2
  32.3 1.4 bitcast_dynamic-update-slice_fusion.2
  34.4 1.4 bitcast_dynamic-update-slice_fusion.2
  36.4 1.4 bitcast_dynamic-update-slice_fusion.2
  40.4 1.4 bitcast_dynamic-update-slice_fusion.2
  41.8 13.4 %multiply_reduce_fusion = (f32[]{:T(128)}, f32[4,4,64,896]{3,2,1,0:T(8,128)}) fusion(bf16[4,2048,896]{2,1,0:T(8,128)(2,1)} %param.10, bf16[4,4,64,2048]{3,2,1,0:T(8,128)(2,1)} %bitcast.34), kind=kOutput, calls=%fused_computation.11 | convolution fusion | flops 3759931392 | bytes 22544388 | tf_op jit(solution)/shard_map/gkir,krc->gkic/dot_general | solution.py:35
  55.2 18.5 %all-reduce.1 = (f32[]{:T(128)}, f32[]{:T(128)}) all-reduce(f32[]{:T(128)} %multiply_reduce_fusion.2, f32[]{:T(128)} %get-tuple-element.32), channel_id=1, replica_groups=mesh['scan'=4,'slab'=8] {'slab'}, use_global_device_ids=true, to_apply=%region_1.0 | all-reduce | flops 2 | bytes 16 | tf_op jit(solution)/shard_map/psum | solution.py:58
  75.1 2.3 %multiply_bitcast_fusion = f32[4,4,64,896]{3,2,0,1:T(8,128)S(1)} fusion(f32[4,4,64,896]{3,2,1,0:T(8,128)} %get-tuple-element.33, f32[]{:T(128)S(6)} %div.6), kind=kLoop, calls=%fused_computation.10 | loop fusion | flops 917504 | bytes 7340036 | tf_op jit(solution)/shard_map/mul | solution.py:66
  77.8 1.7 %copy-done = f32[16,64,896]{2,1,0:T(8,128)S(1)} copy-done((f32[16,64,896]{2,1,0:T(8,128)S(1)}, f32[16,64,896]{2,1,0:T(8,128)}, u32[]{:S(2)}) %copy-start) | copy-done | bytes 3670040
  79.5 2.6 %fusion.14 = (bf16[16,64,896]{2,1,0:T(8,128)(2,1)S(1)}, f32[16,64,896]{2,1,0:T(8,128)}) fusion(f32[16,64,896]{2,1,0:T(8,128)S(1)} %copy-done, f32[4,4,64,896]{3,2,1,0:T(8,128)S(1)} %copy.13), kind=kLoop, calls=%fused_computation.27 | loop fusion | flops 1835008 | bytes 12845056 | tf_op jit(solution)/shard_map/convert_element_type | solution.py:67
  82.1 16.7 %fusion.4 = f32[4,4,64,2048]{3,2,0,1:T(8,128)} fusion(bf16[4,2048,896]{2,1,0:T(8,128)(2,1)} %param.10, bf16[4,4,64,896]{3,2,1,0:T(8,128)(2,1)S(1)} %bitcast.32), kind=kOutput, calls=%fused_computation.7 | convolution fusion | flops 3758096384 | bytes 24903680 | tf_op jit(solution)/shard_map/gkic,krc->gkir/dot_general | solution.py:42
  98.8 7.7 %copy.15 = f32[4,4,64,2048]{3,2,1,0:T(8,128)} copy(f32[4,4,64,2048]{3,2,0,1:T(8,128)} %fusion.4) | data formatting | bytes 16777216 | tf_op jit(solution)/shard_map/gkic,krc->gkir/transpose | solution.py:42
  106.5 15.0 %scatter_custom_fusion = f32[144,2048]{1,0:T(8,128)S(1)} fusion(s32[1024]{0:T(1024)S(1)} %bitcast.33, f32[1024,2048]{1,0:T(8,128)} %bitcast.31, f32[]{:T(128)} %constant.6.clone.1), kind=kCustom, calls=%fused_computation.14 | custom fusion | flops 2097152 | bytes 1180160 | tf_op jit(solution)/shard_map/scatter-add | solution.py:47
  122.9 3.1 %collective-permute-start.3 = (f32[48,2048]{1,0:T(8,128)S(1)}, f32[48,2048]{1,0:T(8,128)S(1)}, u32[]{:S(2)}, u32[]{:S(2)}) collective-permute-start(f32[48,2048]{1,0:T(8,128)S(1)} %get-tuple-element.27), channel_id=1, source_target_pairs={{0,1},{1,2},{2,3},{3,4},{4,5},{5,6},{6,7},{8,9},{9,10},{10,11},{11... | collective-permute-start | bytes 1179656 | tf_op jit(solution)/shard_map/ppermute | solution.py:25
  128.0 17.6 %psum.23 = f32[]{:T(128)} all-reduce(f32[]{:T(128)} %get-tuple-element.22), channel_id=1, replica_groups=mesh['scan'=4,'slab'=8] {'slab'}, use_global_device_ids=true, to_apply=%region_6.0 | all-reduce | flops 1 | bytes 8 | tf_op jit(solution)/shard_map/psum | solution.py:74
  (62 shorter events, 25.7 us)
Async XLA Ops:
  1.7 6.3 %collective-permute-start = (bf16[48,2048]{1,0:T(8,128)(2,1)S(1)}, bf16[48,2048]{1,0:T(8,128)(2,1)S(1)}, u32[]{:S(2)}, u32[]{:S(2)}) collective-permute-start(bf16[48,2048]{1,0:T(8,128)(2,1)S(1)} %convert_element_type.6), channel_id=1, source_target_pairs={{0,1},{1,2},{2,3},{3,4},{4,5},{5,6},{6,7},{8,9},{9,10},{10,11},{11... | collective-permute-start | bytes 589832 | tf_op jit(solution)/shard_map/ppermute | solution.py:14
  4.1 5.5 %collective-permute-start.1 = (bf16[48,2048]{1,0:T(8,128)(2,1)S(1)}, bf16[48,2048]{1,0:T(8,128)(2,1)S(1)}, u32[]{:S(2)}, u32[]{:S(2)}) collective-permute-start(bf16[48,2048]{1,0:T(8,128)(2,1)S(1)} %convert_element_type.6), channel_id=1, source_target_pairs={{1,0},{2,1},{3,2},{4,3},{5,4},{6,5},{7,6},{9,8},{10,9},{11,10},{12... | collective-permute-start | bytes 589832 | tf_op jit(solution)/shard_map/ppermute | solution.py:17
  77.4 2.0 %copy-start = (f32[16,64,896]{2,1,0:T(8,128)S(1)}, f32[16,64,896]{2,1,0:T(8,128)}, u32[]{:S(2)}) copy-start(f32[16,64,896]{2,1,0:T(8,128)} %param.9) | copy-start | bytes 11010052
  106.5 40.5 %copy-start.1 = (f32[48,2048]{1,0:T(8,128)S(1)}, f32[48,2048]{1,0:T(8,128)}, u32[]{:S(2)}) copy-start(f32[48,2048]{1,0:T(8,128)} %param.7) | copy-start | bytes 1179652
  106.5 40.5 %copy-start.3 = (f32[48,2048]{1,0:T(8,128)S(1)}, f32[48,2048]{1,0:T(8,128)}, u32[]{:S(2)}) copy-start(f32[48,2048]{1,0:T(8,128)} %param.6) | copy-start | bytes 1179652
  121.6 4.4 %collective-permute-start.2 = (f32[48,2048]{1,0:T(8,128)S(1)}, f32[48,2048]{1,0:T(8,128)S(1)}, u32[]{:S(2)}, u32[]{:S(2)}) collective-permute-start(f32[48,2048]{1,0:T(8,128)S(1)} %get-tuple-element.26), channel_id=1, source_target_pairs={{1,0},{2,1},{3,2},{4,3},{5,4},{6,5},{7,6},{9,8},{10,9},{11,10},{12... | collective-permute-start | bytes 1179656 | tf_op jit(solution)/shard_map/ppermute | solution.py:25
  122.9 4.4 %collective-permute-start.3 = (f32[48,2048]{1,0:T(8,128)S(1)}, f32[48,2048]{1,0:T(8,128)S(1)}, u32[]{:S(2)}, u32[]{:S(2)}) collective-permute-start(f32[48,2048]{1,0:T(8,128)S(1)} %get-tuple-element.27), channel_id=1, source_target_pairs={{0,1},{1,2},{2,3},{3,4},{4,5},{5,6},{6,7},{8,9},{9,10},{10,11},{11... | collective-permute-start | bytes 1179656 | tf_op jit(solution)/shard_map/ppermute | solution.py:25
  128.0 19.9 %copy-start.2 = (f32[48,2048]{1,0:T(8,128)}, f32[48,2048]{1,0:T(8,128)S(1)}, u32[]{:S(2)}) copy-start(f32[48,2048]{1,0:T(8,128)S(1)} %get-tuple-element.23) | copy-start | bytes 1179652
where the time goes:
time: 149 us; the launch traced here: 148 us
  local copies, waits for them, and re-layouts  42 us (28%)
  blocking collectives  36.2 us (24%)
  matrix products  30.1 us (20%)
  other arithmetic  25.2 us (17%)
  starting transfers between devices  8.05 us (5%)
  between operations  3.45 us (2%)
  waiting for transfers between devices  2.95 us (2%)
    gather x48, local copies, waits for them, and re-layouts  32.1 us
    psum x1, blocking collectives, local(): grad_norm = lax.psum(grad_part, 'slab')  18.5 us
    psum x1, blocking collectives, local(): new_norm = lax.psum(jnp.sum(gradient_next * gradient_next), 'slab')  17.6 us
    dot_general x1, matrix products, backproject(): jnp.einsum('gkic,krc->gkir', grouped, tiles, preferred_element_type=jnp.f...  16.7 us
    scatter-add x1, other arithmetic, backproject(): return accumulated.at[target_rows].add(contribution)  15 us
    dot_general x1, matrix products, project(): jnp.einsum('gkir,krc->gkic', grouped, tiles, preferred_element_type=jnp.f...  13.4 us
    transpose x1, local copies, waits for them, and re-layouts, backproject(): jnp.einsum('gkic,krc->gkir', grouped, tiles, preferred_element_type=jnp.f...  7.7 us
    ppermute x2, starting transfers between devices, from_behind(): return lax.ppermute(block, axis, route)  4.35 us
  transfers between devices with their start and end apart: 4, of which 2 were waited for; matrix products, arithmetic and copies ran while one was open for 2% of the time, Pallas kernels for 0%

commit v1 on v0

v1 whole, which is shorter than its diff:
```python
import functools

import jax
import jax.numpy as jnp
from jax import lax
from jax.experimental import pallas as pl
from jax.experimental.pallas import tpu as pltpu
from jax.sharding import PartitionSpec as P

CHUNK = 256
LANES = 128
VMEM_MIB = 38


def fold_lanes(row):
    total = row[:, :LANES]
    for start in range(LANES, row.shape[1], LANES):
        total = total + row[:, start : start + LANES]
    return total


def kernel(
    count,
    offsets_ref,
    direction_hbm,
    gradient_hbm,
    residual_hbm,
    tiles_hbm,
    residual_out,
    gradient_out,
    stats_out,
    direction_vm,
    gradient_vm,
    residual_vm,
    tiles_vm,
    nearby,
    projected,
    windows,
    hits,
    picks,
    half,
    summed,
    center,
    outgoing,
    incoming,
    stat_send,
    stat_recv,
    stats_vm,
    local_sems,
    tile_sems,
    halo_send,
    halo_recv,
    stat_send_sems,
    stat_recv_sems,
    back_send,
    back_recv,
):
    me = lax.axis_index("slab")
    planes, cells = direction_vm.shape
    views, rows, columns = residual_vm.shape
    angles = tiles_vm.shape[0]
    per_angle = views // angles
    near = 3 * planes
    chunks = cells // CHUNK
    has_low = me > 0
    has_high = me < count - 1

    load_direction = pltpu.make_async_copy(direction_hbm, direction_vm, local_sems.at[0])
    load_gradient = pltpu.make_async_copy(gradient_hbm, gradient_vm, local_sems.at[1])
    load_residual = pltpu.make_async_copy(residual_hbm, residual_vm, local_sems.at[2])

    def load_tile(a):
        return pltpu.make_async_copy(tiles_hbm.at[a], tiles_vm.at[a], tile_sems.at[a])

    load_direction.start()
    for a in range(angles):
        load_tile(a).start()
    load_gradient.start()
    load_residual.start()

    barrier = pltpu.get_barrier_semaphore()
    for d in range(1, count):
        pl.semaphore_signal(barrier, inc=1, device_id={"slab": lax.rem(me + d, count)})

    load_direction.wait()
    nearby[planes : 2 * planes, :] = direction_vm[...].astype(jnp.bfloat16)

    pad = jnp.zeros((planes, cells), jnp.bfloat16)

    @pl.when(jnp.logical_not(has_low))
    def _():
        nearby[:planes, :] = pad
        incoming[:, 1] = jnp.zeros((chunks, planes, CHUNK), jnp.float32)

    @pl.when(jnp.logical_not(has_high))
    def _():
        nearby[2 * planes :, :] = pad
        incoming[:, 0] = jnp.zeros((chunks, planes, CHUNK), jnp.float32)

    pl.semaphore_wait(barrier, count - 1)

    own = nearby.at[pl.ds(planes, planes)]
    to_low = pltpu.make_async_remote_copy(
        own, nearby.at[pl.ds(2 * planes, planes)], halo_send.at[0], halo_recv.at[0],
        device_id={"slab": lax.rem(me + count - 1, count)},
    )
    to_high = pltpu.make_async_remote_copy(
        own, nearby.at[pl.ds(0, planes)], halo_send.at[1], halo_recv.at[1],
        device_id={"slab": lax.rem(me + 1, count)},
    )

    @pl.when(has_low)
    def _():
        to_low.start()

    @pl.when(has_high)
    def _():
        to_high.start()

    plane_id = lax.broadcasted_iota(jnp.int32, (near, per_angle * rows), 0)
    row_id = lax.broadcasted_iota(jnp.int32, (near, per_angle * rows), 1)
    row_of = lax.broadcasted_iota(jnp.int32, (per_angle * rows, near), 0)
    plane_of = lax.broadcasted_iota(jnp.int32, (per_angle * rows, near), 1)
    shift = planes - me * planes
    for a in range(angles):
        base = jnp.zeros_like(row_id)
        for j in range(per_angle):
            first = offsets_ref[j * angles + a] + shift
            base = jnp.where(row_id >= j * rows, first - j * rows, base)
        hits[a] = jnp.where(plane_id == row_id + base, 1.0, 0.0).astype(jnp.bfloat16)
        base = jnp.zeros_like(row_of)
        for j in range(per_angle):
            first = offsets_ref[j * angles + a] + shift
            base = jnp.where(row_of >= j * rows, first - j * rows, base)
        picks[a] = jnp.where(plane_of == row_of + base, 1.0, 0.0).astype(jnp.bfloat16)

    @pl.when(has_low)
    def _():
        to_low.wait_send()
        to_high_recv = to_high
        to_high_recv.wait_recv()

    @pl.when(has_high)
    def _():
        to_high.wait_send()
        to_low.wait_recv()

    def forward(a, total):
        load_tile(a).wait()
        image = jnp.dot(nearby[...], tiles_vm[a], preferred_element_type=jnp.float32)
        upper = image.astype(jnp.bfloat16)
        projected[a, 0] = upper
        projected[a, 1] = (image - upper.astype(jnp.float32)).astype(jnp.bfloat16)
        covering = jnp.sum(hits[a].astype(jnp.float32), axis=1, keepdims=True)
        return total + jnp.sum(image * image * covering, axis=0, keepdims=True)

    image_part = lax.fori_loop(0, angles, forward, jnp.zeros((1, columns), jnp.float32))
    load_gradient.wait()
    grad_part = jnp.sum(gradient_vm[...] * gradient_vm[...], axis=0, keepdims=True)

    def exchange(index):
        copies = []
        for d in range(1, count):
            copies.append(
                pltpu.make_async_remote_copy(
                    stat_send.at[index], stat_recv.at[index, d],
                    stat_send_sems.at[index, d], stat_recv_sems.at[index, d],
                    device_id={"slab": lax.rem(me + d, count)},
                )
            )
        for copy in copies:
            copy.start()
        return copies

    def gather(index, copies):
        total = stat_send[index]
        for d, copy in enumerate(copies):
            copy.wait()
            total = total + stat_recv[index, d + 1]
        return total

    stat_send[0] = jnp.concatenate(
        [fold_lanes(grad_part), fold_lanes(image_part), jnp.zeros((6, LANES), jnp.float32)], axis=0
    )
    copies = exchange(0)

    def pick(a, carry):
        windows[a] = jnp.dot(picks[a], projected[a, 0], preferred_element_type=jnp.float32) + jnp.dot(
            picks[a], projected[a, 1], preferred_element_type=jnp.float32
        )
        return carry

    lax.fori_loop(0, angles, pick, 0)
    load_residual.wait()
    norms = gather(0, copies)
    grad_norm = jnp.sum(norms[0:1], axis=1, keepdims=True)
    image_norm = jnp.sum(norms[1:2], axis=1, keepdims=True)
    step_size = grad_norm / image_norm

    def update(v, carry):
        a = lax.rem(v, angles)
        j = lax.div(v, angles)
        image = windows[a, pl.ds(pl.multiple_of(j * rows, rows), rows), :]
        residual_next = residual_vm[v] - step_size * image
        residual_vm[v] = residual_next
        half[a, pl.ds(pl.multiple_of(j * rows, rows), rows), :] = residual_next.astype(jnp.bfloat16)
        return carry

    lax.fori_loop(0, views, update, 0)
    store_residual = pltpu.make_async_copy(residual_vm, residual_out, local_sems.at[3])
    store_residual.start()

    def gather_rows(a, carry):
        summed[a] = jnp.dot(hits[a], half[a], preferred_element_type=jnp.float32).astype(jnp.bfloat16)
        return carry

    lax.fori_loop(0, angles, gather_rows, 0)

    def back_copy(side, j):
        target = lax.rem(me + (count - 1 if side == 0 else 1), count)
        return pltpu.make_async_remote_copy(
            outgoing.at[j, side], incoming.at[j, side], back_send.at[side, j], back_recv.at[side, j],
            device_id={"slab": target},
        )

    def backward(j, carry):
        cut = pl.ds(pl.multiple_of(j * CHUNK, CHUNK), CHUNK)
        total = jnp.zeros((near, CHUNK), jnp.float32)
        for a in range(angles):
            total = total + lax.dot_general(
                summed[a], tiles_vm[a, cut, :], (((1,), (1,)), ((), ())),
                preferred_element_type=jnp.float32,
            )
        outgoing[j, 0] = total[:planes]
        outgoing[j, 1] = total[2 * planes :]
        center[j] = total[planes : 2 * planes]

        @pl.when(has_low)
        def _():
            back_copy(0, j).start()

        @pl.when(has_high)
        def _():
            back_copy(1, j).start()

        return carry

    lax.fori_loop(0, chunks, backward, 0)

    def combine(j, total):
        @pl.when(has_low)
        def _():
            back_copy(0, j).wait_send()
            back_copy(1, j).wait_recv()

        @pl.when(has_high)
        def _():
            back_copy(1, j).wait_send()
            back_copy(0, j).wait_recv()

        new = center[j] + incoming[j, 0] + incoming[j, 1]
        gradient_vm[:, pl.ds(pl.multiple_of(j * CHUNK, CHUNK), CHUNK)] = new
        return total + jnp.sum(new * new, axis=0, keepdims=True)

    new_part = lax.fori_loop(0, chunks, combine, jnp.zeros((1, CHUNK), jnp.float32))
    stat_send[1] = jnp.concatenate([fold_lanes(new_part), jnp.zeros((7, LANES), jnp.float32)], axis=0)
    copies = exchange(1)
    store_gradient = pltpu.make_async_copy(gradient_vm, gradient_out, local_sems.at[4])
    store_gradient.start()
    new_norm = jnp.sum(gather(1, copies)[0:1], axis=1, keepdims=True)
    stats_vm[...] = jnp.concatenate(
        [
            jnp.broadcast_to(step_size, (1, LANES)),
            jnp.broadcast_to(new_norm / grad_norm, (1, LANES)),
            jnp.zeros((6, LANES), jnp.float32),
        ],
        axis=0,
    )
    store_stats = pltpu.make_async_copy(stats_vm, stats_out, local_sems.at[5])
    store_stats.start()
    store_residual.wait()
    store_gradient.wait()
    store_stats.wait()


def finish(
    stats, solution_ref, direction_ref, gradient_ref, residual_ref,
    solution_out, residual_out, gradient_out, direction_out,
    solution_vm, direction_vm, gradient_vm, sems, residual_vm, residual_in, residual_sems,
):
    pieces = residual_ref.shape[0] // residual_vm.shape[1]
    span = residual_vm.shape[1]

    def part_in(p):
        return pltpu.make_async_copy(
            residual_ref.at[pl.ds(p * span, span)], residual_vm.at[p], residual_in.at[p]
        )

    def part_out(p):
        return pltpu.make_async_copy(
            residual_vm.at[p], residual_out.at[pl.ds(p * span, span)], residual_sems.at[p]
        )

    loads = [
        pltpu.make_async_copy(gradient_ref, gradient_vm, sems.at[0]),
        pltpu.make_async_copy(direction_ref, direction_vm, sems.at[1]),
        pltpu.make_async_copy(solution_ref, solution_vm, sems.at[2]),
    ]
    for p in range(pieces):
        part_in(p).start()
    for load in loads:
        load.start()
    for p in range(pieces):
        part_in(p).wait()
        part_out(p).start()
    for load in loads:
        load.wait()
    stores = [
        pltpu.make_async_copy(gradient_vm, gradient_out, sems.at[3]),
        pltpu.make_async_copy(direction_vm, direction_out, sems.at[4]),
        pltpu.make_async_copy(solution_vm, solution_out, sems.at[5]),
    ]
    stores[0].start()
    solution_vm[...] = solution_vm[...] + stats[0:1, 0:1] * direction_vm[...]
    stores[2].start()
    direction_vm[...] = gradient_vm[...] + stats[1:2, 0:1] * direction_vm[...]
    stores[1].start()
    for store in stores:
        store.wait()
    for p in range(pieces):
        part_out(p).wait()


def local(count, solution, direction, gradient, residual, tiles, offsets):
    planes, cells = solution.shape
    views, rows, columns = residual.shape
    angles = tiles.shape[0]
    per_angle = views // angles
    near = 3 * planes
    chunks = cells // CHUNK
    f32, bf16 = jnp.float32, jnp.bfloat16
    anywhere = pl.BlockSpec(memory_space=pl.ANY)
    residual_next, gradient_next, stats = pl.pallas_call(
        functools.partial(kernel, count),
        name="cgls_step",
        out_shape=(
            jax.ShapeDtypeStruct(residual.shape, f32),
            jax.ShapeDtypeStruct(gradient.shape, f32),
            jax.ShapeDtypeStruct((8, LANES), f32),
        ),
        in_specs=[pl.BlockSpec(memory_space=pltpu.SMEM)] + [anywhere] * 4,
        out_specs=(anywhere,) * 3,
        scratch_shapes=[
            pltpu.VMEM((planes, cells), f32),
            pltpu.VMEM((planes, cells), f32),
            pltpu.VMEM((views, rows, columns), f32),
            pltpu.VMEM((angles, cells, columns), bf16),
            pltpu.VMEM((near, cells), bf16),
            pltpu.VMEM((angles, 2, near, columns), bf16),
            pltpu.VMEM((angles, per_angle * rows, columns), f32),
            pltpu.VMEM((angles, near, per_angle * rows), bf16),
            pltpu.VMEM((angles, per_angle * rows, near), bf16),
            pltpu.VMEM((angles, per_angle * rows, columns), bf16),
            pltpu.VMEM((angles, near, columns), bf16),
            pltpu.VMEM((chunks, planes, CHUNK), f32),
            pltpu.VMEM((chunks, 2, planes, CHUNK), f32),
            pltpu.VMEM((chunks, 2, planes, CHUNK), f32),
            pltpu.VMEM((2, 8, LANES), f32),
            pltpu.VMEM((2, count, 8, LANES), f32),
            pltpu.VMEM((8, LANES), f32),
            pltpu.SemaphoreType.DMA((6,)),
            pltpu.SemaphoreType.DMA((angles,)),
            pltpu.SemaphoreType.DMA((2,)),
            pltpu.SemaphoreType.DMA((2,)),
            pltpu.SemaphoreType.DMA((2, count)),
            pltpu.SemaphoreType.DMA((2, count)),
            pltpu.SemaphoreType.DMA((2, chunks)),
            pltpu.SemaphoreType.DMA((2, chunks)),
        ],
        compiler_params=pltpu.CompilerParams(
            collective_id=0, has_side_effects=True, vmem_limit_bytes=VMEM_MIB * 1024 * 1024
        ),
    )(offsets, direction, gradient, residual, tiles)
    pieces = angles
    volume = jax.ShapeDtypeStruct(solution.shape, f32)
    return pl.pallas_call(
        finish,
        name="finish",
        out_shape=(volume, jax.ShapeDtypeStruct(residual.shape, f32), volume, volume),
        in_specs=[pl.BlockSpec(memory_space=pltpu.VMEM)] + [anywhere] * 4,
        out_specs=(anywhere,) * 4,
        scratch_shapes=[
            pltpu.VMEM((planes, cells), f32),
            pltpu.VMEM((planes, cells), f32),
            pltpu.VMEM((planes, cells), f32),
            pltpu.SemaphoreType.DMA((6,)),
            pltpu.VMEM((pieces, views // pieces, rows, columns), f32),
            pltpu.SemaphoreType.DMA((pieces,)),
            pltpu.SemaphoreType.DMA((pieces,)),
        ],
        compiler_params=pltpu.CompilerParams(vmem_limit_bytes=16 * 1024 * 1024),
    )(stats, solution, direction, gradient_next, residual_next)


def solution(mesh):
    placed = (
        P(("scan", "slab"), None),
        P(("scan", "slab"), None),
        P(("scan", "slab"), None),
        P(("scan", "slab"), None, None),
        P(),
        P(("scan", "slab")),
    )
    return jax.shard_map(
        functools.partial(local, mesh.shape["slab"]),
        mesh=mesh,
        in_specs=placed,
        out_specs=(
            P(("scan", "slab"), None),
            P(("scan", "slab"), None, None),
            P(("scan", "slab"), None),
            P(("scan", "slab"), None),
        ),
        check_vma=False,
    )
```

time: 149 us -> 40.5 us (0.27)
  local copies, waits for them, and re-layouts: 42 us -> 4.68 us
  blocking collectives: 36.2 us -> 0 us
  Pallas kernels: 0 us -> 34.9 us
  matrix products: 30.1 us -> 0 us
  other arithmetic: 25.2 us -> 0 us
  starting transfers between devices: 8.05 us -> 0 us
  waiting for transfers between devices: 2.95 us -> 0 us
  between operations: 3.45 us -> 0.66 us
    psum x2 -> x0, blocking collectives: 36.2 us -> none  [the longest x1 18.5 us: local(): grad_norm = lax.psum(grad_part, 'slab')]
    pallas_call x0 -> x2, Pallas kernels: none -> 34.9 us  [the longest x1 31.1 us: local(): pl.pallas_call(functools.partial(kernel, count), name='cgls_step', out_sh...]
    gather x48 -> x0, local copies, waits for them, and re-layouts: 32.1 us -> none
    dot_general x2 -> x0, matrix products: 30.1 us -> none  [the longest x1 16.7 us: backproject(): jnp.einsum('gkic,krc->gkir', grouped, tiles, preferred_element_type=jnp.f...]
    scatter-add x1 -> x0, other arithmetic: 15 us -> none  [backproject(): return accumulated.at[target_rows].add(contribution)]
    ppermute x4 -> x0, starting transfers between devices: 8.05 us -> none  [the longest x2 4.35 us: from_behind(): return lax.ppermute(block, axis, route)]
    transpose x1 -> x0, local copies, waits for them, and re-layouts: 7.7 us -> none  [backproject(): jnp.einsum('gkic,krc->gkir', grouped, tiles, preferred_element_type=jnp.f...]
    convert_element_type x2 -> x0, other arithmetic: 3.62 us -> none  [the longest x1 2.6 us: local(): residual_half = residual_next.astype(jnp.bfloat16)]
  transfers between devices with their start and end apart: 4 -> 0, of which waited for: 2 -> 0; matrix products, arithmetic and copies ran while one was open for 2% -> 0% of each run, Pallas kernels for 0% -> 0%
where the time goes in v1:
time: 40.5 us; the launch traced here: 40.3 us
  Pallas kernels  34.9 us (86%)
  local copies, waits for them, and re-layouts  4.68 us (12%)
  between operations  0.66 us (2%)
    pallas_call x1, Pallas kernels, local(): pl.pallas_call(functools.partial(kernel, count), name='cgls_step', out_sh...  31.1 us
    unnamed x10, local copies, waits for them, and re-layouts  4.68 us
    pallas_call x1, Pallas kernels, local(): pl.pallas_call(finish, name='finish', out_shape=(volume, jax.ShapeDtypeSt...  3.79 us

profile of v1, /device:TPU:0, one launch (start us, length us, event | category | flops | bytes accessed | tf_op | source)
XLA Modules:
  0.0 40.3 jit_solution(3580992983580587624)
XLA Ops:
  0.6 0.0 copy-start
  0.6 2.0 %copy-done = f32[16,64,896]{2,1,0:T(8,128)S(1)} copy-done((f32[16,64,896]{2,1,0:T(8,128)S(1)}, f32[16,64,896]{2,1,0:T(8,128)}, u32[]{:S(2)}) %copy-start) | copy-done | bytes 3670040
  2.7 0.0 copy-start.1
  2.7 1.0 %copy-done.1 = f32[48,2048]{1,0:T(8,128)S(1)} copy-done((f32[48,2048]{1,0:T(8,128)S(1)}, f32[48,2048]{1,0:T(8,128)}, u32[]{:S(2)}) %copy-start.1) | copy-done | bytes 393240
  3.7 0.0 copy-start.2
  3.7 1.0 %copy-done.2 = f32[48,2048]{1,0:T(8,128)S(1)} copy-done((f32[48,2048]{1,0:T(8,128)S(1)}, f32[48,2048]{1,0:T(8,128)}, u32[]{:S(2)}) %copy-start.2) | copy-done | bytes 393240
  4.7 0.0 copy-start.4
  4.7 0.7 %copy-done.4 = s32[16]{0:T(128)S(1)} copy-done((s32[16]{0:T(128)S(1)}, s32[16]{0:T(128)}, u32[]{:S(2)}) %copy-start.4) | copy-done | bytes 88
  5.3 0.0 copy-start.3
  5.3 31.1 %cgls_step.1 = (f32[16,64,896]{2,1,0:T(8,128)S(1)}, f32[48,2048]{1,0:T(8,128)S(1)}, f32[8,128]{1,0:T(8,128)S(1)}) custom-call(s32[16]{0:T(128)S(1)} %copy-done.4, f32[48,2048]{1,0:T(8,128)S(1)} %copy-done.1, f32[48,2048]{1,0:T(8,128)S(1)} %copy-done.2, f32[16,64,896]{2,1,0:T(8,128)S(1)} %copy-done, bf16[4,2048,896]{2,1,0:T(8,128)(2,1)} %tiles_hbm.1), custom_call_target="tpu_custom_call" | custom-call | tf_op jit(solution)/shard_map/cgls_step/pallas_call | solution.py:343
  36.5 0.0 copy-done.3
  36.5 3.8 %finish.1 = (f32[48,2048]{1,0:T(8,128)}, f32[16,64,896]{2,1,0:T(8,128)}, f32[48,2048]{1,0:T(8,128)}, f32[48,2048]{1,0:T(8,128)}) custom-call(f32[8,128]{1,0:T(8,128)S(1)} %get-tuple-element.7.stats, f32[48,2048]{1,0:T(8,128)S(1)} %copy-done.3, f32[48,2048]{1,0:T(8,128)S(1)} %copy-done.1, f32[48,2048]{1,0:T(8,128)S(1)} %get-tuple-element.8.gradient_ref, ...), custom_call_target="tpu_custom_call" | custom-call | tf_op jit(solution)/shard_map/finish/pallas_call | solution.py:386
Async XLA Ops:
  0.6 2.0 %copy-start = (f32[16,64,896]{2,1,0:T(8,128)S(1)}, f32[16,64,896]{2,1,0:T(8,128)}, u32[]{:S(2)}) copy-start(f32[16,64,896]{2,1,0:T(8,128)} %residual_hbm.1) | copy-start | bytes 11010052
  2.7 1.0 %copy-start.1 = (f32[48,2048]{1,0:T(8,128)S(1)}, f32[48,2048]{1,0:T(8,128)}, u32[]{:S(2)}) copy-start(f32[48,2048]{1,0:T(8,128)} %direction_ref.1) | copy-start | bytes 1179652
  3.7 1.0 %copy-start.2 = (f32[48,2048]{1,0:T(8,128)S(1)}, f32[48,2048]{1,0:T(8,128)}, u32[]{:S(2)}) copy-start(f32[48,2048]{1,0:T(8,128)} %gradient_hbm.1) | copy-start | bytes 1179652
  4.7 0.7 %copy-start.4 = (s32[16]{0:T(128)S(1)}, s32[16]{0:T(128)}, u32[]{:S(2)}) copy-start(s32[16]{0:T(128)} %offsets_ref.1) | copy-start | bytes 196
  5.3 31.1 %copy-start.3 = (f32[48,2048]{1,0:T(8,128)S(1)}, f32[48,2048]{1,0:T(8,128)}, u32[]{:S(2)}) copy-start(f32[48,2048]{1,0:T(8,128)} %solution_ref.1) | copy-start | bytes 1179652
